TPU v7x, 32 devices: a whole 2x2x4 slice. The times are simulated.
32 devices in a mesh: dp: 2 (over x), fsdp: 8 (over z, y), seq: 2 (over core).
Axes of the slice: x: 2, y: 2, z: 4, core: 2. Of those that a mesh axis runs over, the one named last changes fastest.
Arguments:
- tokens_in: bfloat16 [16, 1040, 1024], P(('dp', 'fsdp'), 'seq'), may hold values from -6 to 6
- key_mask: int32 [16, 1040], P(('dp', 'fsdp')), may hold values from 0 to 1, as said below
- attn_weights: bfloat16 [2, 1024, 4096], P(None, 'fsdp')
- mlp_weights: bfloat16 [2, 1024, 8192], P(None, 'fsdp')
- vectors: bfloat16 [2, 14, 1024], P(None, None, 'fsdp')
- cotangent: bfloat16 [16, 1040, 1024], P(('dp', 'fsdp'), 'seq'), may hold values from -6 to 6
- first_attn: float32 [2, 1024, 4096], P(None, 'fsdp'), may hold values from -40 to 40
- second_attn: float32 [2, 1024, 4096], P(None, 'fsdp'), may hold values from 0.832 to 8.32
- first_mlp: float32 [2, 1024, 8192], P(None, 'fsdp'), may hold values from -40 to 40
- second_mlp: float32 [2, 1024, 8192], P(None, 'fsdp'), may hold values from 0.832 to 8.32
- first_vec: float32 [2, 14, 1024], P(None, None, 'fsdp'), may hold values from -80 to 80
- second_vec: float32 [2, 14, 1024], P(None, None, 'fsdp'), may hold values from 3.328 to 33.28
Outputs:
- tokens_out: float32 [16, 1040, 1024], P(('dp', 'fsdp'), 'seq')
- grad_tokens: float32 [16, 1040, 1024], P(('dp', 'fsdp'), 'seq')
- grad_attn: float32 [2, 1024, 4096], P(None, 'fsdp')
- grad_mlp: float32 [2, 1024, 8192], P(None, 'fsdp')
- grad_vectors: float32 [2, 14, 1024], P(None, None, 'fsdp')
- step_attn: float32 [2, 1024, 4096], P(None, 'fsdp')
- step_mlp: float32 [2, 1024, 8192], P(None, 'fsdp')
- step_vectors: float32 [2, 14, 1024], P(None, None, 'fsdp')
- new_first_attn: float32 [2, 1024, 4096], P(None, 'fsdp')
- new_second_attn: float32 [2, 1024, 4096], P(None, 'fsdp')
- new_first_mlp: float32 [2, 1024, 8192], P(None, 'fsdp')
- new_second_mlp: float32 [2, 1024, 8192], P(None, 'fsdp')
- new_first_vec: float32 [2, 14, 1024], P(None, None, 'fsdp')
- new_second_vec: float32 [2, 14, 1024], P(None, None, 'fsdp')
Inputs may be any that keep to these rules, and one draw needn't show every extreme that they name: `key_mask`: each image's row is 1 on its first slots and 0 on the rest; at least 910 ones and at least one 0 in every row.
All inputs are finite; a program needn't handle non-finite values.
Results may differ from a plain program's by a relative error of at most 0.023.
Values may be sent and summed in bfloat16 or wider, within the bound.
No kernel may reach another device: no remote copies, remote signals or barrier semaphores. Data moves between devices by JAX's collectives and lax.ppermute only.
A program may use at most 320 MiB of HBM per device.

v0:
```python
import jax
import jax.numpy as jnp
from jax import lax
from jax.sharding import PartitionSpec as P

HD = 64
norm_eps = 1e-06
neg_large = -1e30
beta_first = 0.9
beta_second = 0.999
adam_eps = 1e-08
decay_rate = 0.05
rate_matrix = 0.01
rate_vector = 0.05
step_count = 10.0


def layer_norm(values, norm_gain, norm_shift):
    center = values - jnp.mean(values, axis=-1, keepdims=True)
    spread = jnp.mean(center * center, axis=-1, keepdims=True)
    return center * lax.rsqrt(spread + norm_eps) * norm_gain + norm_shift


def gelu_exact(values):
    return jax.nn.gelu(values, approximate=False)


def contract_last(left_side, right_side):
    return lax.dot_general(
        left_side,
        right_side,
        (((left_side.ndim - 1,), (1,)), ((), ())),
        preferred_element_type=jnp.float32,
    )


def contract_rows(left_side, right_side):
    return lax.dot_general(
        left_side, right_side, (((0, 1), (0, 1)), ((), ())), preferred_element_type=jnp.float32
    )


def masked_scores(query_rows, key_rows, valid_keys):
    scores = contract_last(query_rows, key_rows) * query_rows.shape[-1] ** (-0.5)
    return jnp.where(valid_keys[None, :] > 0, scores, neg_large)


def attend_item(item_set):
    query_rows, key_rows, value_rows, valid_keys = item_set
    scores = masked_scores(query_rows, key_rows, valid_keys)
    row_top = jnp.max(scores, axis=-1, keepdims=True)
    exp_terms = jnp.exp(scores - row_top)
    row_total = jnp.sum(exp_terms, axis=-1, keepdims=True)
    attention = (exp_terms / row_total).astype(jnp.bfloat16)
    mixed_rows = jnp.dot(attention, value_rows, preferred_element_type=jnp.float32)
    return (mixed_rows.astype(jnp.bfloat16), row_top[:, 0] + jnp.log(row_total[:, 0]))


def attend_back(item_set):
    query_rows, key_rows, value_rows, valid_keys, log_total, grad_rows = item_set
    score_scale = query_rows.shape[-1] ** (-0.5)
    scores = masked_scores(query_rows, key_rows, valid_keys)
    attention = jnp.exp(scores - log_total[:, None])
    grad_value = lax.dot_general(
        attention.astype(jnp.bfloat16),
        grad_rows,
        (((0,), (0,)), ((), ())),
        preferred_element_type=jnp.float32,
    )
    grad_attention = contract_last(grad_rows, value_rows)
    inner_sum = jnp.sum(attention * grad_attention, axis=-1, keepdims=True)
    grad_scores = (attention * (grad_attention - inner_sum)).astype(jnp.bfloat16)
    grad_query = jnp.dot(grad_scores, key_rows, preferred_element_type=jnp.float32) * score_scale
    grad_key = (
        lax.dot_general(
            grad_scores, query_rows, (((0,), (0,)), ((), ())), preferred_element_type=jnp.float32
        )
        * score_scale
    )
    return jnp.stack([grad_query, grad_key, grad_value]).astype(jnp.bfloat16)


def forward_layer(inputs, mask_heads, attn_full, mlp_full, vectors_full):
    model_width = attn_full.shape[0]
    hidden = mlp_full.shape[1] // 2
    vec_rows = vectors_full.astype(jnp.float32)
    n_seq = lax.axis_size("seq")
    images, token_rows, _ = inputs.shape
    length = token_rows * n_seq
    group_width = model_width // n_seq
    per_group = group_width // HD
    normed = layer_norm(inputs, vec_rows[0], vec_rows[1]).astype(jnp.bfloat16)
    bias_qkv = jnp.concatenate([vec_rows[2], jnp.zeros_like(vec_rows[2]), vec_rows[3]])
    qkv = (
        jnp.dot(normed, attn_full[:, : 3 * model_width], preferred_element_type=jnp.float32)
        + bias_qkv
    ).astype(jnp.bfloat16)
    heads = lax.all_to_all(
        qkv.reshape(images, token_rows, 3, n_seq, group_width),
        "seq",
        split_axis=3,
        concat_axis=1,
        tiled=True,
    )
    stacked = (
        heads.reshape(images, length, 3, per_group, HD)
        .transpose(2, 0, 3, 1, 4)
        .reshape(3, images * per_group, length, HD)
    )
    mixed_items, log_total = lax.map(attend_item, (stacked[0], stacked[1], stacked[2], mask_heads))
    mixed_heads = (
        mixed_items.reshape(images, per_group, length, HD)
        .transpose(0, 2, 1, 3)
        .reshape(images, length, 1, group_width)
    )
    mixed_rows = lax.all_to_all(
        mixed_heads, "seq", split_axis=1, concat_axis=2, tiled=True
    ).reshape(images, token_rows, model_width)
    branch = contract_last(mixed_rows, attn_full[:, 3 * model_width :]) + vec_rows[4]
    middle = inputs + vec_rows[5] * branch
    normed_two = layer_norm(middle, vec_rows[6], vec_rows[7]).astype(jnp.bfloat16)
    pre_act = jnp.dot(
        normed_two, mlp_full[:, :hidden], preferred_element_type=jnp.float32
    ) + vec_rows[10:].reshape(hidden)
    active = gelu_exact(pre_act).astype(jnp.bfloat16)
    mlp_out = contract_last(active, mlp_full[:, hidden:]) + vec_rows[8]
    output = middle + vec_rows[9] * mlp_out
    saved_set = (
        inputs,
        normed,
        stacked,
        log_total,
        mixed_rows,
        branch,
        middle,
        normed_two,
        pre_act,
        active,
        mlp_out,
    )
    return (output, saved_set)


def backward_layer(upstream, saved_set, attn_full, mlp_full, vectors_full, mask_heads):
    (
        inputs,
        normed,
        stacked,
        log_total,
        mixed_rows,
        branch,
        middle,
        normed_two,
        pre_act,
        active,
        mlp_out,
    ) = saved_set
    model_width = attn_full.shape[0]
    hidden = mlp_full.shape[1] // 2
    vec_rows = vectors_full.astype(jnp.float32)
    n_seq = lax.axis_size("seq")
    images, token_rows, _ = upstream.shape
    length = token_rows * n_seq
    group_width = model_width // n_seq
    per_group = group_width // HD
    grad_scale_two = jnp.sum(upstream * mlp_out, axis=(0, 1))
    grad_mlp_out = (upstream * vec_rows[9]).astype(jnp.bfloat16)
    grad_bias_down = jnp.sum(grad_mlp_out.astype(jnp.float32), axis=(0, 1))
    grad_down = contract_rows(grad_mlp_out, active)
    grad_active = jnp.dot(grad_mlp_out, mlp_full[:, hidden:], preferred_element_type=jnp.float32)
    _, gelu_pull = jax.vjp(gelu_exact, pre_act)
    grad_pre = gelu_pull(grad_active)[0].astype(jnp.bfloat16)
    grad_bias_up = jnp.sum(grad_pre.astype(jnp.float32), axis=(0, 1))
    grad_up = contract_rows(normed_two, grad_pre)
    grad_normed_two = contract_last(grad_pre, mlp_full[:, :hidden])
    _, second_pull = jax.vjp(layer_norm, middle, vec_rows[6], vec_rows[7])
    grad_mid_norm, grad_gain_two, grad_shift_two = second_pull(grad_normed_two)
    grad_middle = upstream + grad_mid_norm
    grad_scale_one = jnp.sum(grad_middle * branch, axis=(0, 1))
    grad_branch = (grad_middle * vec_rows[5]).astype(jnp.bfloat16)
    grad_bias_proj = jnp.sum(grad_branch.astype(jnp.float32), axis=(0, 1))
    grad_proj = contract_rows(grad_branch, mixed_rows)
    grad_mixed = jnp.dot(
        grad_branch, attn_full[:, 3 * model_width :], preferred_element_type=jnp.float32
    ).astype(jnp.bfloat16)
    grad_heads = lax.all_to_all(
        grad_mixed.reshape(images, token_rows, n_seq, group_width),
        "seq",
        split_axis=2,
        concat_axis=1,
        tiled=True,
    )
    grad_items = (
        grad_heads.reshape(images, length, per_group, HD)
        .transpose(0, 2, 1, 3)
        .reshape(images * per_group, length, HD)
    )
    grad_stack = lax.map(
        attend_back, (stacked[0], stacked[1], stacked[2], mask_heads, log_total, grad_items)
    )
    grad_stack = (
        grad_stack.reshape(images, per_group, 3, length, HD)
        .transpose(0, 3, 2, 1, 4)
        .reshape(images, length, 3, 1, group_width)
    )
    grad_qkv = lax.all_to_all(grad_stack, "seq", split_axis=1, concat_axis=3, tiled=True).reshape(
        images, token_rows, 3 * model_width
    )
    grad_qkv_sum = jnp.sum(grad_qkv.astype(jnp.float32), axis=(0, 1))
    grad_qkv_weight = contract_rows(normed, grad_qkv)
    grad_normed = contract_last(grad_qkv, attn_full[:, : 3 * model_width])
    _, first_pull = jax.vjp(layer_norm, inputs, vec_rows[0], vec_rows[1])
    grad_in_norm, grad_gain_one, grad_shift_one = first_pull(grad_normed)
    grad_inputs = grad_middle + grad_in_norm
    grad_attn = jnp.concatenate([grad_qkv_weight, grad_proj], axis=1)
    grad_mlp = jnp.concatenate([grad_up, grad_down], axis=1)
    grad_rows = jnp.stack(
        [
            grad_gain_one,
            grad_shift_one,
            grad_qkv_sum[:model_width],
            grad_qkv_sum[2 * model_width :],
            grad_bias_proj,
            grad_scale_one,
            grad_gain_two,
            grad_shift_two,
            grad_bias_down,
            grad_scale_two,
        ]
    )
    grad_vec = jnp.concatenate(
        [grad_rows, grad_bias_up.reshape(hidden // model_width, model_width)], axis=0
    )
    return (grad_inputs, (grad_attn, grad_mlp, grad_vec))


def adam_step(weights, gradient, moment_one, moment_two, step_rate, decay_weight):
    one_new = beta_first * moment_one + (1.0 - beta_first) * gradient
    two_new = beta_second * moment_two + (1.0 - beta_second) * gradient * gradient
    one_hat = one_new / (1.0 - beta_first**step_count)
    two_hat = two_new / (1.0 - beta_second**step_count)
    change = -step_rate * (
        one_hat / (jnp.sqrt(two_hat) + adam_eps) + decay_weight * weights.astype(jnp.float32)
    )
    return (change, one_new, two_new)


def local(
    tokens_in,
    key_mask,
    attn_weights,
    mlp_weights,
    vectors,
    cotangent,
    first_attn,
    second_attn,
    first_mlp,
    second_mlp,
    first_vec,
    second_vec,
):
    layers = attn_weights.shape[0]
    n_seq = lax.axis_size("seq")
    per_group = attn_weights.shape[2] // 4 // n_seq // HD
    mask_heads = jnp.repeat(key_mask, per_group, axis=0)
    residual = tokens_in.astype(jnp.float32)
    stored = []
    gathered_sets = []
    for layer_index in range(layers):
        weight_set = (
            lax.all_gather(attn_weights[layer_index], "fsdp", axis=0, tiled=True),
            lax.all_gather(mlp_weights[layer_index], "fsdp", axis=0, tiled=True),
            lax.all_gather(vectors[layer_index], "fsdp", axis=1, tiled=True),
        )
        residual, saved_set = forward_layer(
            residual, mask_heads, weight_set[0], weight_set[1], weight_set[2]
        )
        stored.append(saved_set)
        gathered_sets.append(weight_set)
    upstream = cotangent.astype(jnp.float32)
    layer_grads = [None] * layers
    for layer_index in reversed(range(layers)):
        weight_set = (
            lax.all_gather(attn_weights[layer_index], "fsdp", axis=0, tiled=True),
            lax.all_gather(mlp_weights[layer_index], "fsdp", axis=0, tiled=True),
            lax.all_gather(vectors[layer_index], "fsdp", axis=1, tiled=True),
        )
        upstream, local_grads = backward_layer(
            upstream, stored[layer_index], weight_set[0], weight_set[1], weight_set[2], mask_heads
        )
        owned = (
            lax.psum_scatter(
                local_grads[0].astype(jnp.bfloat16), "fsdp", scatter_dimension=0, tiled=True
            ).astype(jnp.float32),
            lax.psum_scatter(
                local_grads[1].astype(jnp.bfloat16), "fsdp", scatter_dimension=0, tiled=True
            ).astype(jnp.float32),
            lax.psum_scatter(
                local_grads[2].astype(jnp.bfloat16), "fsdp", scatter_dimension=1, tiled=True
            ).astype(jnp.float32),
        )
        owned = (
            lax.psum(owned[0].astype(jnp.bfloat16), ("dp", "seq")).astype(jnp.float32),
            lax.psum(owned[1].astype(jnp.bfloat16), ("dp", "seq")).astype(jnp.float32),
            lax.psum(owned[2].astype(jnp.bfloat16), ("dp", "seq")).astype(jnp.float32),
        )
        layer_grads[layer_index] = owned
    grad_attn = jnp.stack([layer_grads[index_one][0] for index_one in range(layers)])
    grad_mlp = jnp.stack([layer_grads[index_one][1] for index_one in range(layers)])
    grad_vectors = jnp.stack([layer_grads[index_one][2] for index_one in range(layers)])
    step_attn, one_attn, two_attn = adam_step(
        attn_weights, grad_attn, first_attn, second_attn, rate_matrix, decay_rate
    )
    step_mlp, one_mlp, two_mlp = adam_step(
        mlp_weights, grad_mlp, first_mlp, second_mlp, rate_matrix, decay_rate
    )
    step_vectors, one_vec, two_vec = adam_step(
        vectors, grad_vectors, first_vec, second_vec, rate_vector, 0.0
    )
    return (
        residual,
        upstream,
        grad_attn,
        grad_mlp,
        grad_vectors,
        step_attn,
        step_mlp,
        step_vectors,
        one_attn,
        two_attn,
        one_mlp,
        two_mlp,
        one_vec,
        two_vec,
    )


def solution(mesh):
    return jax.shard_map(
        local,
        mesh=mesh,
        in_specs=(
            P(("dp", "fsdp"), "seq", None),
            P(("dp", "fsdp"), None),
            P(None, "fsdp", None),
            P(None, "fsdp", None),
            P(None, None, "fsdp"),
            P(("dp", "fsdp"), "seq", None),
            P(None, "fsdp", None),
            P(None, "fsdp", None),
            P(None, "fsdp", None),
            P(None, "fsdp", None),
            P(None, None, "fsdp"),
            P(None, None, "fsdp"),
        ),
        out_specs=(
            P(("dp", "fsdp"), "seq", None),
            P(("dp", "fsdp"), "seq", None),
            P(None, "fsdp", None),
            P(None, "fsdp", None),
            P(None, None, "fsdp"),
            P(None, "fsdp", None),
            P(None, "fsdp", None),
            P(None, None, "fsdp"),
            P(None, "fsdp", None),
            P(None, "fsdp", None),
            P(None, "fsdp", None),
            P(None, "fsdp", None),
            P(None, None, "fsdp"),
            P(None, None, "fsdp"),
        ),
        check_vma=False,
    )
```

profile of v0, /device:TPU:0, one launch (start us, length us, event | category | flops | bytes accessed | tf_op | source)
XLA Modules:
  0.0 2304.5 jit_solution(1958127319763447503)
XLA Ops:
  16.5 23.2 %all-gather = bf16[1,14,1024]{2,0,1:T(2,128)(2,1)S(1)} all-gather(bf16[1,14,128]{2,0,1:T(2,128)(2,1)S(1)} %get-tuple-element.468), channel_id=2, replica_groups=mesh['dp'=2,'fsdp'=8,'seq'=2] {'fsdp'}, dimensions={2}, use_global_device_ids=true | all-gather | bytes 32256 | tf_op jit(solution)/shard_map/all_gather | solution.py:273
  39.9 17.4 all-gather.3
  59.9 79.7 %all-gather.11.cloned.1.call-done = bf16[1,1024,4096]{2,1,0:T(8,128)(2,1)} async-done(((bf16[1,128,4096]{2,1,0:T(8,128)(2,1)}), bf16[1,1024,4096]{2,1,0:T(8,128)(2,1)}) %all-gather.11.cloned.1.call-update) | async-done | bytes 8388624 | tf_op jit(solution)/shard_map/all_gather | solution.py:271
  139.5 8.1 add_convert_fusion.3
  147.6 8.5 reshape.862
  158.6 7.5 all_to_all.120
  166.1 10.3 copy.103
  176.4 8.6 reshape.863
  198.8 72.4 %while.44 = (s32[]{:T(128)}, bf16[8,1040,64]{1,2,0:T(8,128)(2,1)}, f32[8,1040]{1,0:T(8,128)S(1)}, s32[8,1040]{1,0:T(8,128)S(1)}, bf16[8,1040,64]{2,1,0:T(8,128)(...) while((s32[]{:T(128)}, bf16[8,1040,64]{1,2,0:T(8,128)(2,1)}, ...), condition=%wide.region_5.6_spmd, body=%wide.region_2.5_spmd.sunk | while | flops 285608960 | bytes 31756240 | solution.py:110
  271.2 6.4 copy.107
  278.2 8.9 reduce.63
  289.4 7.1 all_to_all.121
  299.9 4.7 fusion.226
  305.0 63.0 %all-gather.13.cloned.1.call-done = bf16[1,1024,8192]{2,1,0:T(8,128)(2,1)} async-done(((bf16[1,128,8192]{2,1,0:T(8,128)(2,1)}), bf16[1,1024,8192]{2,1,0:T(8,128)(2,1)}) %all-gather.13.cloned.1.call-update) | async-done | bytes 16777232 | tf_op jit(solution)/shard_map/all_gather | solution.py:272
  368.1 27.1 %multiply_convert_fusion.3 = (bf16[520,4096]{1,0:T(8,128)(2,1)S(1)}, f32[520,4096]{1,0:T(8,128)}, f32[520,4096]{1,0:T(8,128)}) fusion(f32[4096]{0:T(1024)S(1)} %bitcast.487, bf16[1024,8192]{1,0:T(8,128)(2,1)} %bitcast.522, f32[1,520,1024]{2,1,0:T(8,128)S(1)} %get-tuple-element.424, f32[1024]{0:T(1024)S(1)} %bitcast.513, f32[1024]{0:T(1024)S(1)} %bitcast.499, ...), kind=kOutput, calls=%fused_computation.138 | convolution fusion | flops 4505313280 | bytes 31846464 | tf_op jit(solution)/shard_map/dot_general | solution.py:122
  395.3 11.5 fusion.224
  407.2 86.7 %all-gather.15.cloned.1.call-done = bf16[1,1024,4096]{2,1,0:T(8,128)(2,1)} async-done(((bf16[1,128,4096]{2,1,0:T(8,128)(2,1)}), bf16[1,1024,4096]{2,1,0:T(8,128)(2,1)}) %all-gather.15.cloned.1.call-update) | async-done | bytes 8388624 | tf_op jit(solution)/shard_map/all_gather | solution.py:271
  493.9 8.0 add_convert_fusion.2
  502.0 8.6 reshape.869
  513.0 7.5 all_to_all.122
  520.5 10.3 copy.110
  530.7 8.6 reshape.870
  552.9 68.8 %while.45 = (s32[]{:T(128)}, bf16[8,1040,64]{1,2,0:T(8,128)(2,1)S(1)}, f32[8,1040]{1,0:T(8,128)S(1)}, s32[8,1040]{1,0:T(8,128)S(1)}, bf16[8,1040,64]{2,1,0:T(8,1...) while((s32[]{:T(128)}, ...), condition=%wide.region_13.14_spmd, body=%wide.region_10.13_spmd.sunk | while | flops 285608960 | bytes 31763296 | solution.py:110
  625.8 8.9 reduce.64
  636.2 5.6 all_to_all.123
  647.8 4.7 fusion.223
  654.4 67.8 %all-gather.17.cloned.1.call-done = bf16[1,1024,8192]{2,1,0:T(8,128)(2,1)} async-done(((bf16[1,128,8192]{2,1,0:T(8,128)(2,1)}), bf16[1,1024,8192]{2,1,0:T(8,128)(2,1)}) %all-gather.17.cloned.1.call-update) | async-done | bytes 16777232 | tf_op jit(solution)/shard_map/all_gather | solution.py:272
  722.3 28.0 %multiply_convert_fusion.2 = (bf16[520,4096]{1,0:T(8,128)(2,1)}, f32[520,4096]{1,0:T(8,128)}, f32[520,4096]{1,0:T(8,128)}) fusion(f32[4096]{0:T(1024)S(1)} %bitcast.489, bf16[1024,8192]{1,0:T(8,128)(2,1)} %bitcast.526, f32[1,520,1024]{2,1,0:T(8,128)} %copy-done.8, f32[1024]{0:T(1024)S(1)} %bitcast.511, f32[1024]{0:T(1024)S(1)} %bitcast.495, ...), kind=kOutput, calls=%fused_computation.125 | convolution fusion | flops 4505313280 | bytes 31846464 | tf_op jit(solution)/shard_map/dot_general | solution.py:122
  750.4 14.5 fusion.234
  764.9 9.6 fusion.153
  792.1 99.1 %while.46 = (s32[]{:T(128)}, bf16[8,3,1040,64]{2,3,1,0:T(8,128)(2,1)S(1)}, s32[8,1040]{1,0:T(8,128)}, bf16[8,1040,64]{2,1,0:T(8,128)(2,1)}, bf16[8,1040,64]{2,1,...) while((s32[]{:T(128)}, ...), condition=%wide.region_20.21_spmd, body=%wide.region_18.20_spmd.sunk | while | flops 703489280 | bytes 35388936 | solution.py:198
  893.3 8.4 copy.123
  901.8 8.7 all_to_all.125
  917.1 8.5 reshape.882
  925.7 7.9 fusion.155
  937.0 14.5 fusion.152
  952.4 14.3 fusion.235
  966.7 10.0 fusion.157
  997.4 99.1 %while.47 = (s32[]{:T(128)}, bf16[8,3,1040,64]{2,3,1,0:T(8,128)(2,1)S(1)}, s32[8,1040]{1,0:T(8,128)}, bf16[8,1040,64]{2,1,0:T(8,128)(2,1)}, bf16[8,1040,64]{2,1,...) while((s32[]{:T(128)}, ...), condition=%wide.region_27.28_spmd, body=%wide.region_25.27_spmd.sunk | while | flops 703489280 | bytes 35388936 | solution.py:198
  1098.7 8.4 copy.133
  1107.1 8.7 all_to_all.127
  1122.4 8.4 reshape.890
  1130.9 9.4 convolution_convert_fusion.5
  1140.3 7.0 pad_maximum_fusion.2
  1147.4 4.9 convolution_convert_fusion.6
  1152.3 7.7 convolution_convert_fusion.4
  1160.1 7.8 pad_maximum_fusion.3
  1167.9 9.1 convolution_convert_fusion.2
  1177.0 9.6 convolution_convert_fusion.3
  1186.6 6.6 pad_maximum_fusion
  1193.9 9.3 convolution_convert_fusion
  1203.3 9.6 convolution_convert_fusion.1
  1212.9 6.6 pad_maximum_fusion.1
  1219.6 6.9 fusion.150
  1237.8 56.8 %reduce-scatter.11.cloned.1.call-done = bf16[128,4096]{1,0:T(8,128)(2,1)} async-done(((bf16[1024,4096]{1,0:T(8,128)(2,1)}), bf16[128,4096]{1,0:T(8,128)(2,1)}) %reduce-scatter.11.cloned.1.call-update) | async-done | bytes 1048592 | tf_op jit(solution)/shard_map/reduce_scatter | solution.py:292
  1294.7 152.5 %reduce-scatter.13.cloned.1.call-done = bf16[128,4096]{1,0:T(8,128)(2,1)} async-done(((bf16[1024,4096]{1,0:T(8,128)(2,1)}), bf16[128,4096]{1,0:T(8,128)(2,1)}) %reduce-scatter.13.cloned.1.call-update) | async-done | bytes 1048592 | tf_op jit(solution)/shard_map/reduce_scatter | solution.py:292
  1447.2 285.6 %reduce-scatter.15.cloned.1.call-done = bf16[128,8192]{1,0:T(8,128)(2,1)} async-done(((bf16[1024,8192]{1,0:T(8,128)(2,1)}), bf16[128,8192]{1,0:T(8,128)(2,1)}) %reduce-scatter.15.cloned.1.call-update) | async-done | bytes 2097168 | tf_op jit(solution)/shard_map/reduce_scatter | solution.py:295
  1732.8 286.1 %reduce-scatter.17.cloned.1.call-done = bf16[128,8192]{1,0:T(8,128)(2,1)} async-done(((bf16[1024,8192]{1,0:T(8,128)(2,1)}), bf16[128,8192]{1,0:T(8,128)(2,1)}) %reduce-scatter.17.cloned.1.call-update) | async-done | bytes 2097168 | tf_op jit(solution)/shard_map/reduce_scatter | solution.py:295
  2022.6 60.4 %reduce-scatter.19.cloned.1.call-done = bf16[128,14]{1,0:T(8,128)(2,1)} async-done(((bf16[1024,14]{1,0:T(8,128)(2,1)}), bf16[128,14]{1,0:T(8,128)(2,1)}) %reduce-scatter.19.cloned.1.call-update) | async-done | bytes 3600
  2083.9 63.2 %reduce-scatter.21.cloned.1.call-done = bf16[128,14]{1,0:T(8,128)(2,1)} async-done(((bf16[1024,14]{1,0:T(8,128)(2,1)}), bf16[128,14]{1,0:T(8,128)(2,1)}) %reduce-scatter.21.cloned.1.call-update) | async-done | bytes 3600
  2147.9 5.8 all-reduce
  2156.2 112.7 %all-reduce.4.cloned.1.call-done = (bf16[1,128,4096]{2,1,0:T(8,128)(2,1)}, bf16[1,128,4096]{2,1,0:T(8,128)(2,1)}, bf16[1,128,8192]{2,1,0:T(8,128)(2,1)}, bf16[1,128,8192]{2,1,0:T(8,128)(2,1)}) async-done(((bf16[1,128,4096]{2,1,0:T(8,128)(2,1)}, bf16[1,128,4096]{2,1,0:T(8,128)(2,1)}, bf16[1,128,8192]{2,1,0:T(8,128)(2,1)}, bf16[1,128,8192]{2,1,0:T(8,128)(2,1)}), (bf16[1,128,4096]{2,1,0:T(8,128)(2,1)}, ...) | async-done | bytes 6291472 | tf_op jit(solution)/shard_map/psum | solution.py:303
  2268.9 19.0 add_multiply_fusion
  2288.0 9.8 add_multiply_fusion.1
  (680 shorter events, 481.9 us)
Async XLA Ops:
  7.2 132.3 %all-gather.11.cloned.1.call-start = ((), (), s32[]{:S(2)}) async-start(), calls=%async_computation.18 | async-start | bytes 9437184 | tf_op jit(solution)/shard_map/all_gather | solution.py:271
  10.3 357.7 %all-gather.13.cloned.1.call-start = ((), (), s32[]{:S(2)}) async-start(), calls=%async_computation.19 | async-start | bytes 18874368 | tf_op jit(solution)/shard_map/all_gather | solution.py:272
  15.1 43.5 %copy-start.16 = (bf16[1,520,1024]{2,1,0:T(8,128)(2,1)S(1)}, bf16[1,520,1024]{2,1,0:T(8,128)(2,1)}, u32[]{:S(2)}) copy-start(bf16[1,520,1024]{2,1,0:T(8,128)(2,1)} %param.20) | copy-start | bytes 3194884
  15.1 44.1 %copy-start.101 = (s32[1,1040]{1,0:T(1,128)S(1)}, s32[1,1040]{1,0:T(1,128)}, u32[]{:S(2)}) copy-start(s32[1,1040]{1,0:T(1,128)} %param.21) | copy-start | bytes 12484
  15.1 478.8 %all-gather.15.cloned.1.call-start = ((), (), s32[]{:S(2)}) async-start(), calls=%async_computation.20 | async-start | bytes 9437184 | tf_op jit(solution)/shard_map/all_gather | solution.py:271
  15.8 706.5 %all-gather.17.cloned.1.call-start = ((), (), s32[]{:S(2)}) async-start(), calls=%async_computation.21 | async-start | bytes 18874368 | tf_op jit(solution)/shard_map/all_gather | solution.py:272
  16.4 1278.3 %reduce-scatter.11.cloned.1.call-start = ((), (), s32[]{:S(2)}) async-start(), calls=%async_computation.14 | async-start | bytes 9437184 | tf_op jit(solution)/shard_map/reduce_scatter | solution.py:292
  39.7 107.9 %copy-start.49 = (f32[1,1,1024]{2,0,1:T(1,128)}, f32[1,1,1024]{2,0,1:T(1,128)S(1)}, u32[]{:S(2)}) copy-start(f32[1,1,1024]{2,0,1:T(1,128)S(1)} %get-tuple-element.463) | copy-start | bytes 12292
  39.8 107.8 %copy-start.106 = (f32[1,1,1024]{2,0,1:T(1,128)}, f32[1,1,1024]{2,0,1:T(1,128)S(1)}, u32[]{:S(2)}) copy-start(f32[1,1,1024]{2,0,1:T(1,128)S(1)} %get-tuple-element.464) | copy-start | bytes 12292
  39.8 260.1 %copy-start.66 = (f32[1,1,1024]{2,0,1:T(1,128)}, f32[1,1,1024]{2,0,1:T(1,128)S(1)}, u32[]{:S(2)}) copy-start(f32[1,1,1024]{2,0,1:T(1,128)S(1)} %get-tuple-element.461) | copy-start | bytes 12292
  39.8 260.1 %copy-start.68 = (f32[1,1,1024]{2,0,1:T(1,128)}, f32[1,1,1024]{2,0,1:T(1,128)S(1)}, u32[]{:S(2)}) copy-start(f32[1,1,1024]{2,0,1:T(1,128)S(1)} %get-tuple-element.462) | copy-start | bytes 12292
  39.8 328.3 %copy-start.77 = (f32[1,1,1024]{2,0,1:T(1,128)}, f32[1,1,1024]{2,0,1:T(1,128)S(1)}, u32[]{:S(2)}) copy-start(f32[1,1,1024]{2,0,1:T(1,128)S(1)} %get-tuple-element.459) | copy-start | bytes 12292
  39.8 328.3 %copy-start.104 = (f32[1,1,1024]{2,0,1:T(1,128)}, f32[1,1,1024]{2,0,1:T(1,128)S(1)}, u32[]{:S(2)}) copy-start(f32[1,1,1024]{2,0,1:T(1,128)S(1)} %get-tuple-element.460) | copy-start | bytes 12292
  39.8 355.4 %copy-start.70 = (f32[1,1,1024]{2,0,1:T(1,128)}, f32[1,1,1024]{2,0,1:T(1,128)S(1)}, u32[]{:S(2)}) copy-start(f32[1,1,1024]{2,0,1:T(1,128)S(1)} %get-tuple-element.457) | copy-start | bytes 12292
  39.8 355.4 %copy-start.110 = (f32[1,1,1024]{2,0,1:T(1,128)}, f32[1,1,1024]{2,0,1:T(1,128)S(1)}, u32[]{:S(2)}) copy-start(f32[1,1,1024]{2,0,1:T(1,128)S(1)} %get-tuple-element.458) | copy-start | bytes 12292
  39.9 328.2 %copy-start.72 = (f32[1,4,1024]{2,0,1:T(1,128)}, f32[1,4,1024]{2,0,1:T(1,128)S(1)}, u32[]{:S(2)}) copy-start(f32[1,4,1024]{2,0,1:T(1,128)S(1)} %slice.263) | copy-start | bytes 49156
  58.7 88.9 %copy-start.42 = (f32[520]{0:T(1024)}, f32[520]{0:T(1024)S(1)}, u32[]{:S(2)}) copy-start(f32[520]{0:T(1024)S(1)} %broadcast_multiply_fusion.3) | copy-start | bytes 6244
  59.2 88.4 %copy-start.51 = (f32[520]{0:T(1024)}, f32[520]{0:T(1024)S(1)}, u32[]{:S(2)}) copy-start(f32[520]{0:T(1024)S(1)} %fusion.149) | copy-start | bytes 6244
  59.2 88.4 %copy-start.44 = (f32[520]{0:T(1024)}, f32[520]{0:T(1024)S(1)}, u32[]{:S(2)}) copy-start(f32[520]{0:T(1024)S(1)} %fusion.199) | copy-start | bytes 6244
  271.2 15.9 copy-start.15
  271.2 15.9 copy-start.40
  304.6 90.6 %copy-start.19 = (f32[1,520,1024]{2,1,0:T(8,128)}, f32[1,520,1024]{2,1,0:T(8,128)S(1)}, u32[]{:S(2)}) copy-start(f32[1,520,1024]{2,1,0:T(8,128)S(1)} %get-tuple-element.424) | copy-start | bytes 6389764
  304.6 90.6 %copy-start.57 = (f32[520]{0:T(1024)}, f32[520]{0:T(1024)S(1)}, u32[]{:S(2)}) copy-start(f32[520]{0:T(1024)S(1)} %broadcast_multiply_fusion.2) | copy-start | bytes 6244
  305.0 90.2 %copy-start.53 = (f32[520]{0:T(1024)}, f32[520]{0:T(1024)S(1)}, u32[]{:S(2)}) copy-start(f32[520]{0:T(1024)S(1)} %multiply_reduce_fusion.4) | copy-start | bytes 6244
  305.0 90.2 %copy-start.84 = (f32[520]{0:T(1024)}, f32[520]{0:T(1024)S(1)}, u32[]{:S(2)}) copy-start(f32[520]{0:T(1024)S(1)} %fusion.200) | copy-start | bytes 6244
  395.2 11.6 copy-start.119
  395.3 98.6 %copy-start.81 = (f32[1,1,1024]{2,0,1:T(1,128)S(1)}, f32[1,1,1024]{2,0,1:T(1,128)}, u32[]{:S(2)}) copy-start(f32[1,1,1024]{2,0,1:T(1,128)} %get-tuple-element.453) | copy-start | bytes 12292
  395.3 98.6 %copy-start.93 = (f32[3072]{0:T(1024)S(1)}, f32[3072]{0:T(1024)}, u32[]{:S(2)}) copy-start(f32[3072]{0:T(1024)} %get-tuple-element.473) | copy-start | bytes 36868
  395.3 98.6 %copy-start.108 = (f32[1,1,1024]{2,0,1:T(1,128)S(1)}, f32[1,1,1024]{2,0,1:T(1,128)}, u32[]{:S(2)}) copy-start(f32[1,1,1024]{2,0,1:T(1,128)} %get-tuple-element.454) | copy-start | bytes 12292
  406.8 240.9 %copy-start.5 = (f32[1,520,1024]{2,1,0:T(8,128)}, f32[1,520,1024]{2,1,0:T(8,128)S(1)}, u32[]{:S(2)}) copy-start(f32[1,520,1024]{2,1,0:T(8,128)S(1)} %get-tuple-element.420) | copy-start | bytes 6389764
  406.8 95.1 %copy-start.59 = (f32[520]{0:T(1024)}, f32[520]{0:T(1024)S(1)}, u32[]{:S(2)}) copy-start(f32[520]{0:T(1024)S(1)} %broadcast_multiply_fusion.1) | copy-start | bytes 6244
  407.2 94.8 %copy-start.55 = (f32[520]{0:T(1024)}, f32[520]{0:T(1024)S(1)}, u32[]{:S(2)}) copy-start(f32[520]{0:T(1024)S(1)} %multiply_reduce_fusion.3) | copy-start | bytes 6244
  407.2 94.7 %copy-start.86 = (f32[520]{0:T(1024)}, f32[520]{0:T(1024)S(1)}, u32[]{:S(2)}) copy-start(f32[520]{0:T(1024)S(1)} %fusion.201) | copy-start | bytes 6244
  621.7 13.1 copy-start.39
  621.7 13.1 copy-start.41
  647.8 74.5 %copy-start.74 = (f32[1,4,1024]{2,0,1:T(1,128)S(1)}, f32[1,4,1024]{2,0,1:T(1,128)}, u32[]{:S(2)}) copy-start(f32[1,4,1024]{2,0,1:T(1,128)} %slice.281) | copy-start | bytes 49156
  647.8 74.5 %copy-start.75 = (f32[1,1,1024]{2,0,1:T(1,128)S(1)}, f32[1,1,1024]{2,0,1:T(1,128)}, u32[]{:S(2)}) copy-start(f32[1,1,1024]{2,0,1:T(1,128)} %get-tuple-element.449) | copy-start | bytes 12292
  647.8 74.5 %copy-start.102 = (f32[1,1,1024]{2,0,1:T(1,128)S(1)}, f32[1,1,1024]{2,0,1:T(1,128)}, u32[]{:S(2)}) copy-start(f32[1,1,1024]{2,0,1:T(1,128)} %get-tuple-element.450) | copy-start | bytes 12292
  652.6 122.0 %copy-start.62 = (f32[520]{0:T(1024)}, f32[520]{0:T(1024)S(1)}, u32[]{:S(2)}) copy-start(f32[520]{0:T(1024)S(1)} %broadcast_multiply_fusion) | copy-start | bytes 6244
  654.4 120.1 %copy-start.89 = (f32[520]{0:T(1024)}, f32[520]{0:T(1024)S(1)}, u32[]{:S(2)}) copy-start(f32[520]{0:T(1024)S(1)} %fusion.202) | copy-start | bytes 6244
  722.3 28.1 %copy-start.34 = (bf16[1,520,1024]{2,1,0:T(8,128)(2,1)S(1)}, bf16[1,520,1024]{2,1,0:T(8,128)(2,1)}, u32[]{:S(2)}) copy-start(bf16[1,520,1024]{2,1,0:T(8,128)(2,1)} %param.25) | copy-start | bytes 3194884
  722.3 28.1 %copy-start.79 = (f32[1,1,1024]{2,0,1:T(1,128)S(1)}, f32[1,1,1024]{2,0,1:T(1,128)}, u32[]{:S(2)}) copy-start(f32[1,1,1024]{2,0,1:T(1,128)} %get-tuple-element.447) | copy-start | bytes 12292
  750.4 14.6 copy-start.9
  937.0 14.5 copy-start.71
  952.4 14.3 copy-start.37
  952.4 14.3 copy-start.20
  952.4 14.3 copy-start.58
  952.4 14.3 copy-start.78
  952.4 14.3 copy-start.85
  966.7 10.1 copy-start.121
  966.7 10.1 copy-start.54
  1147.4 299.8 %reduce-scatter.13.cloned.1.call-start = ((), (), s32[]{:S(2)}) async-start(), calls=%async_computation.15 | async-start | bytes 9437184 | tf_op jit(solution)/shard_map/reduce_scatter | solution.py:292
  1167.9 564.9 %reduce-scatter.15.cloned.1.call-start = ((), (), s32[]{:S(2)}) async-start(), calls=%async_computation.16 | async-start | bytes 18874368 | tf_op jit(solution)/shard_map/reduce_scatter | solution.py:295
  1193.3 825.6 %reduce-scatter.17.cloned.1.call-start = ((), (), s32[]{:S(2)}) async-start(), calls=%async_computation.17 | async-start | bytes 18874368 | tf_op jit(solution)/shard_map/reduce_scatter | solution.py:295
  1219.5 863.6 %reduce-scatter.19.cloned.1.call-start = ((), (), s32[]{:S(2)}) async-start(), calls=%async_computation.22 | async-start | bytes 294912
  1234.0 913.1 %reduce-scatter.21.cloned.1.call-start = ((), (), s32[]{:S(2)}) async-start(), calls=%async_computation.23 | async-start | bytes 294912
  1237.6 781.4 %copy-start.13 = (f32[520,1024]{1,0:T(8,128)S(1)}, f32[520,1024]{1,0:T(8,128)}, u32[]{:S(2)}) copy-start(f32[520,1024]{1,0:T(8,128)} %copy-done.12) | copy-start | bytes 6389764
  1237.6 781.4 %copy-start.18 = (bf16[1,520,1024]{2,1,0:T(8,128)(2,1)S(1)}, bf16[1,520,1024]{2,1,0:T(8,128)(2,1)}, u32[]{:S(2)}) copy-start(bf16[1,520,1024]{2,1,0:T(8,128)(2,1)} %param.20) | copy-start | bytes 3194884
  1237.6 1031.3 %all-reduce.4.cloned.1.call-start = ((), (), s32[]{:S(2)}) async-start(), calls=%async_computation.24 | async-start | bytes 12582912 | tf_op jit(solution)/shard_map/psum | solution.py:303
  2019.0 134.8 %copy-start.47 = (bf16[2,14,128]{2,0,1:T(2,128)(2,1)S(1)}, bf16[2,14,128]{2,0,1:T(2,128)(2,1)}, u32[]{:S(2)}) copy-start(bf16[2,14,128]{2,0,1:T(2,128)(2,1)} %param.24) | copy-start | bytes 21508
  2019.0 134.8 %copy-start.91 = (f32[2,14,128]{2,0,1:T(2,128)S(1)}, f32[2,14,128]{2,0,1:T(2,128)}, u32[]{:S(2)}) copy-start(f32[2,14,128]{2,0,1:T(2,128)} %param.30) | copy-start | bytes 43012
  2019.0 134.8 %copy-start.92 = (f32[2,14,128]{2,0,1:T(2,128)S(1)}, f32[2,14,128]{2,0,1:T(2,128)}, u32[]{:S(2)}) copy-start(f32[2,14,128]{2,0,1:T(2,128)} %param.31) | copy-start | bytes 43012
  2268.9 19.0 copy-start.27
  2268.9 19.1 copy-start.38
  (83 other events, 363.0 us)
Sparse Core Ops, SparseCore 0:
  10.7 128.7 all-gather.10
  142.2 225.7 all-gather.12
  370.8 123.1 all-gather.14
  496.5 225.7 all-gather.16
  1147.5 147.1 reduce-scatter.10
  1299.2 147.9 reduce-scatter.12
  1451.0 281.8 reduce-scatter.14
  1737.1 281.7 reduce-scatter.16
  2022.8 60.2 reduce-scatter.18
  2086.8 60.2 reduce-scatter.20
  2149.7 119.1 all-reduce.3
where the time goes:
time: 2320 us; the launch traced here: 2300 us
  waiting for transfers between devices  1320 us (57%)
  matrix products  486 us (21%)
  local copies, waits for them, and re-layouts  247 us (11%)
  other arithmetic  136 us (6%)
  blocking collectives  101 us (4%)
    reduce_scatter x2, waiting for transfers between devices, local(): lax.psum_scatter(local_grads[1].astype(jnp.bfloat16), 'fsdp', scatter_dim...  572 us
    reduce_scatter x2, waiting for transfers between devices, local(): lax.psum_scatter(local_grads[0].astype(jnp.bfloat16), 'fsdp', scatter_dim...  209 us
    dot_general x56, matrix products, contract_last(): lax.dot_general(left_side, right_side, (((left_side.ndim - 1,), (1,)), ((...  176 us
    all_gather x2, waiting for transfers between devices, local(): lax.all_gather(attn_weights[layer_index], 'fsdp', axis=0, tiled=True)  166 us
    all_gather x2, waiting for transfers between devices, local(): lax.all_gather(mlp_weights[layer_index], 'fsdp', axis=0, tiled=True)  131 us
    unnamed x13, waiting for transfers between devices  125 us
    psum x1, waiting for transfers between devices, local(): lax.psum(owned[0].astype(jnp.bfloat16), ('dp', 'seq')).astype(jnp.float32)  113 us
    dot_general x8, matrix products, contract_rows(): lax.dot_general(left_side, right_side, (((0, 1), (0, 1)), ((), ())), pref...  62.7 us
  transfers between devices with their start and end apart: 11, of which 11 were waited for; matrix products, arithmetic and copies ran while one was open for 17% of the time, Pallas kernels for 0%

commit v1 on v0

--- a/solution.py
+++ b/solution.py
@@ -299,8 +299,12 @@
                 local_grads[2].astype(jnp.bfloat16), "fsdp", scatter_dimension=1, tiled=True
             ).astype(jnp.float32),
         )
+
+        def render_hubs(sample, named_axis):
+            return lax.all_gather(sample, axis_name=named_axis).sum(axis=0)
+
         owned = (
-            lax.psum(owned[0].astype(jnp.bfloat16), ("dp", "seq")).astype(jnp.float32),
+            render_hubs(owned[0].astype(jnp.bfloat16), ("dp", "seq")).astype(jnp.float32),
             lax.psum(owned[1].astype(jnp.bfloat16), ("dp", "seq")).astype(jnp.float32),
             lax.psum(owned[2].astype(jnp.bfloat16), ("dp", "seq")).astype(jnp.float32),
         )

time: 2320 us -> 2340 us (level)
    all_gather x0 -> x2, waiting for transfers between devices: none -> 58.8 us  [render_hubs(): return lax.all_gather(sample, axis_name=named_axis).sum(axis=0)]
    psum x1, waiting for transfers between devices: 113 us -> 74.1 us  [local(): lax.psum(owned[1].astype(jnp.bfloat16), ('dp', 'seq')).astype(jnp.float32)]
    unnamed x13 -> x15, waiting for transfers between devices: 125 us -> 125 us
  transfers between devices with their start and end apart: 11 -> 13, of which waited for: 11 -> 13; matrix products, arithmetic and copies ran while one was open for 17% -> 18% of each run, Pallas kernels for 0% -> 0%
where the time goes in v1:
time: 2340 us; the launch traced here: 2330 us
  waiting for transfers between devices  1340 us (57%)
  matrix products  486 us (21%)
  local copies, waits for them, and re-layouts  247 us (11%)
  other arithmetic  143 us (6%)
  blocking collectives  101 us (4%)
    reduce_scatter x2, waiting for transfers between devices, local(): lax.psum_scatter(local_grads[1].astype(jnp.bfloat16), 'fsdp', scatter_dim...  571 us
    reduce_scatter x2, waiting for transfers between devices, local(): lax.psum_scatter(local_grads[0].astype(jnp.bfloat16), 'fsdp', scatter_dim...  209 us
    dot_general x56, matrix products, contract_last(): lax.dot_general(left_side, right_side, (((left_side.ndim - 1,), (1,)), ((...  176 us
    all_gather x2, waiting for transfers between devices, local(): lax.all_gather(attn_weights[layer_index], 'fsdp', axis=0, tiled=True)  166 us
    all_gather x2, waiting for transfers between devices, local(): lax.all_gather(mlp_weights[layer_index], 'fsdp', axis=0, tiled=True)  131 us
    unnamed x15, waiting for transfers between devices  125 us
    psum x1, waiting for transfers between devices, local(): lax.psum(owned[1].astype(jnp.bfloat16), ('dp', 'seq')).astype(jnp.float32)  74.1 us
    dot_general x8, matrix products, contract_rows(): lax.dot_general(left_side, right_side, (((0, 1), (0, 1)), ((), ())), pref...  62.7 us
  transfers between devices with their start and end apart: 13, of which 13 were waited for; matrix products, arithmetic and copies ran while one was open for 18% of the time, Pallas kernels for 0%

profile of v1, /device:TPU:0, one launch (start us, length us, event | category | flops | bytes accessed | tf_op | source)
XLA Modules:
  0.0 2331.6 jit_solution(16864770279141808231)
XLA Ops:
  16.5 23.2 all-gather
  39.9 17.4 all-gather.3
  59.9 79.7 %all-gather.15.cloned.1.call-done = bf16[1,1024,4096]{2,1,0:T(8,128)(2,1)} async-done(((bf16[1,128,4096]{2,1,0:T(8,128)(2,1)}), bf16[1,1024,4096]{2,1,0:T(8,128)(2,1)}) %all-gather.15.cloned.1.call-update) | async-done | bytes 8388624 | tf_op jit(solution)/shard_map/all_gather | solution.py:271
  139.5 8.1 add_convert_fusion.3
  147.6 8.5 reshape.880
  158.6 7.5 all_to_all.120
  166.1 10.2 copy.103
  176.4 8.6 reshape.881
  198.8 72.5 %while.44 = (s32[]{:T(128)}, bf16[8,1040,64]{1,2,0:T(8,128)(2,1)}, f32[8,1040]{1,0:T(8,128)S(1)}, s32[8,1040]{1,0:T(8,128)S(1)}, bf16[8,1040,64]{2,1,0:T(8,128)(...) while((s32[]{:T(128)}, bf16[8,1040,64]{1,2,0:T(8,128)(2,1)}, ...), condition=%wide.region_5.6_spmd, body=%wide.region_2.5_spmd.sunk | while | flops 285608960 | bytes 31756240 | solution.py:110
  271.3 6.4 copy.107
  278.1 8.9 reduce.65
  289.3 7.1 all_to_all.121
  304.9 63.2 %all-gather.17.cloned.1.call-done = bf16[1,1024,8192]{2,1,0:T(8,128)(2,1)} async-done(((bf16[1,128,8192]{2,1,0:T(8,128)(2,1)}), bf16[1,1024,8192]{2,1,0:T(8,128)(2,1)}) %all-gather.17.cloned.1.call-update) | async-done | bytes 16777232 | tf_op jit(solution)/shard_map/all_gather | solution.py:272
  368.1 27.0 %multiply_convert_fusion.3 = (bf16[520,4096]{1,0:T(8,128)(2,1)S(1)}, f32[520,4096]{1,0:T(8,128)}, f32[520,4096]{1,0:T(8,128)}) fusion(f32[4096]{0:T(1024)S(1)} %bitcast.491, bf16[1024,8192]{1,0:T(8,128)(2,1)} %bitcast.526, f32[1,520,1024]{2,1,0:T(8,128)S(1)} %get-tuple-element.422, f32[1024]{0:T(1024)S(1)} %bitcast.517, f32[1024]{0:T(1024)S(1)} %bitcast.503, ...), kind=kOutput, calls=%fused_computation.138 | convolution fusion | flops 4505313280 | bytes 31846464 | tf_op jit(solution)/shard_map/dot_general | solution.py:122
  395.2 11.5 fusion.224
  407.1 86.8 %all-gather.19.cloned.1.call-done = bf16[1,1024,4096]{2,1,0:T(8,128)(2,1)} async-done(((bf16[1,128,4096]{2,1,0:T(8,128)(2,1)}), bf16[1,1024,4096]{2,1,0:T(8,128)(2,1)}) %all-gather.19.cloned.1.call-update) | async-done | bytes 8388624 | tf_op jit(solution)/shard_map/all_gather | solution.py:271
  493.9 8.0 add_convert_fusion.2
  502.0 8.6 reshape.887
  513.0 7.5 all_to_all.122
  520.5 10.2 copy.110
  530.7 8.6 reshape.888
  552.9 68.8 %while.45 = (s32[]{:T(128)}, bf16[8,1040,64]{1,2,0:T(8,128)(2,1)S(1)}, f32[8,1040]{1,0:T(8,128)S(1)}, s32[8,1040]{1,0:T(8,128)S(1)}, bf16[8,1040,64]{2,1,0:T(8,1...) while((s32[]{:T(128)}, ...), condition=%wide.region_13.14_spmd, body=%wide.region_10.13_spmd.sunk | while | flops 285608960 | bytes 31763296 | solution.py:110
  625.8 8.9 reduce.66
  636.2 5.6 all_to_all.123
  654.3 67.9 %all-gather.21.cloned.1.call-done = bf16[1,1024,8192]{2,1,0:T(8,128)(2,1)} async-done(((bf16[1,128,8192]{2,1,0:T(8,128)(2,1)}), bf16[1,1024,8192]{2,1,0:T(8,128)(2,1)}) %all-gather.21.cloned.1.call-update) | async-done | bytes 16777232 | tf_op jit(solution)/shard_map/all_gather | solution.py:272
  722.3 28.0 %multiply_convert_fusion.2 = (bf16[520,4096]{1,0:T(8,128)(2,1)}, f32[520,4096]{1,0:T(8,128)}, f32[520,4096]{1,0:T(8,128)}) fusion(f32[4096]{0:T(1024)S(1)} %bitcast.493, bf16[1024,8192]{1,0:T(8,128)(2,1)} %bitcast.530, f32[1,520,1024]{2,1,0:T(8,128)} %copy-done.8, f32[1024]{0:T(1024)S(1)} %bitcast.515, f32[1024]{0:T(1024)S(1)} %bitcast.499, ...), kind=kOutput, calls=%fused_computation.125 | convolution fusion | flops 4505313280 | bytes 31846464 | tf_op jit(solution)/shard_map/dot_general | solution.py:122
  750.4 14.5 fusion.234
  764.9 9.6 fusion.153
  792.1 99.1 %while.46 = (s32[]{:T(128)}, bf16[8,3,1040,64]{2,3,1,0:T(8,128)(2,1)S(1)}, s32[8,1040]{1,0:T(8,128)}, bf16[8,1040,64]{2,1,0:T(8,128)(2,1)}, bf16[8,1040,64]{2,1,...) while((s32[]{:T(128)}, ...), condition=%wide.region_20.21_spmd, body=%wide.region_18.20_spmd.sunk | while | flops 703489280 | bytes 35388936 | solution.py:198
  893.4 8.4 copy.123
  901.8 8.7 all_to_all.125
  917.2 8.5 reshape.900
  925.7 7.9 fusion.155
  937.0 14.4 fusion.152
  952.4 14.3 fusion.235
  966.7 10.0 fusion.157
  997.2 99.1 %while.47 = (s32[]{:T(128)}, bf16[8,3,1040,64]{2,3,1,0:T(8,128)(2,1)S(1)}, s32[8,1040]{1,0:T(8,128)}, bf16[8,1040,64]{2,1,0:T(8,128)(2,1)}, bf16[8,1040,64]{2,1,...) while((s32[]{:T(128)}, ...), condition=%wide.region_27.28_spmd, body=%wide.region_25.27_spmd.sunk | while | flops 703489280 | bytes 35388936 | solution.py:198
  1098.5 8.4 copy.133
  1107.0 8.7 all_to_all.127
  1122.3 8.4 reshape.908
  1130.7 9.4 convolution_convert_fusion.5
  1140.2 7.0 pad_maximum_fusion.2
  1147.3 4.9 convolution_convert_fusion.6
  1152.2 7.7 convolution_convert_fusion.4
  1159.9 7.8 pad_maximum_fusion.3
  1167.8 9.1 convolution_convert_fusion.2
  1176.9 9.6 convolution_convert_fusion.3
  1186.5 6.6 pad_maximum_fusion
  1193.8 9.3 convolution_convert_fusion
  1203.1 9.6 convolution_convert_fusion.1
  1212.7 6.6 pad_maximum_fusion.1
  1219.4 6.8 fusion.150
  1237.5 56.9 %reduce-scatter.11.cloned.1.call-done = bf16[128,4096]{1,0:T(8,128)(2,1)} async-done(((bf16[1024,4096]{1,0:T(8,128)(2,1)}), bf16[128,4096]{1,0:T(8,128)(2,1)}) %reduce-scatter.11.cloned.1.call-update) | async-done | bytes 1048592 | tf_op jit(solution)/shard_map/reduce_scatter | solution.py:292
  1294.6 152.3 %reduce-scatter.13.cloned.1.call-done = bf16[128,4096]{1,0:T(8,128)(2,1)} async-done(((bf16[1024,4096]{1,0:T(8,128)(2,1)}), bf16[128,4096]{1,0:T(8,128)(2,1)}) %reduce-scatter.13.cloned.1.call-update) | async-done | bytes 1048592 | tf_op jit(solution)/shard_map/reduce_scatter | solution.py:292
  1447.0 285.4 %reduce-scatter.15.cloned.1.call-done = bf16[128,8192]{1,0:T(8,128)(2,1)} async-done(((bf16[1024,8192]{1,0:T(8,128)(2,1)}), bf16[128,8192]{1,0:T(8,128)(2,1)}) %reduce-scatter.15.cloned.1.call-update) | async-done | bytes 2097168 | tf_op jit(solution)/shard_map/reduce_scatter | solution.py:295
  1732.4 286.0 %reduce-scatter.17.cloned.1.call-done = bf16[128,8192]{1,0:T(8,128)(2,1)} async-done(((bf16[1024,8192]{1,0:T(8,128)(2,1)}), bf16[128,8192]{1,0:T(8,128)(2,1)}) %reduce-scatter.17.cloned.1.call-update) | async-done | bytes 2097168 | tf_op jit(solution)/shard_map/reduce_scatter | solution.py:295
  2022.2 60.6 %reduce-scatter.19.cloned.1.call-done = bf16[128,14]{1,0:T(8,128)(2,1)} async-done(((bf16[1024,14]{1,0:T(8,128)(2,1)}), bf16[128,14]{1,0:T(8,128)(2,1)}) %reduce-scatter.19.cloned.1.call-update) | async-done | bytes 3600
  2083.6 63.3 %reduce-scatter.21.cloned.1.call-done = bf16[128,14]{1,0:T(8,128)(2,1)} async-done(((bf16[1024,14]{1,0:T(8,128)(2,1)}), bf16[128,14]{1,0:T(8,128)(2,1)}) %reduce-scatter.21.cloned.1.call-update) | async-done | bytes 3600
  2147.6 5.8 all-reduce
  2155.9 26.0 %all-gather.23.cloned.1.call-done = bf16[512,4096]{1,0:T(8,128)(2,1)} async-done(((bf16[128,4096]{1,0:T(8,128)(2,1)}), bf16[512,4096]{1,0:T(8,128)(2,1)}) %all-gather.23.cloned.1.call-update) | async-done | bytes 4194320 | tf_op jit(solution)/shard_map/all_gather | solution.py:304
  2185.0 32.9 %all-gather.25.cloned.1.call-done = bf16[512,4096]{1,0:T(8,128)(2,1)} async-done(((bf16[128,4096]{1,0:T(8,128)(2,1)}), bf16[512,4096]{1,0:T(8,128)(2,1)}) %all-gather.25.cloned.1.call-update) | async-done | bytes 4194320 | tf_op jit(solution)/shard_map/all_gather | solution.py:304
  2222.1 9.8 add_multiply_fusion.1
  2231.9 74.1 %all-reduce.4.cloned.1.call-done = (bf16[1,128,8192]{2,1,0:T(8,128)(2,1)}, bf16[1,128,8192]{2,1,0:T(8,128)(2,1)}) async-done(((bf16[1,128,8192]{2,1,0:T(8,128)(2,1)}, bf16[1,128,8192]{2,1,0:T(8,128)(2,1)}), (bf16[1,128,8192]{2,1,0:T(8,128)(2,1)}, bf16[1,128,8192]{2,1,0:T(8,128)(2,1)})) %all-reduce.4.cloned.1.call-update) | async-done | bytes 4194320 | tf_op jit(solution)/shard_map/psum | solution.py:308
  2306.0 18.9 add_multiply_fusion
  (686 shorter events, 498.6 us)
Async XLA Ops:
  7.2 132.3 %all-gather.15.cloned.1.call-start = ((), (), s32[]{:S(2)}) async-start(), calls=%async_computation.18 | async-start | bytes 9437184 | tf_op jit(solution)/shard_map/all_gather | solution.py:271
  10.3 357.7 %all-gather.17.cloned.1.call-start = ((), (), s32[]{:S(2)}) async-start(), calls=%async_computation.19 | async-start | bytes 18874368 | tf_op jit(solution)/shard_map/all_gather | solution.py:272
  15.1 43.5 %copy-start.16 = (bf16[1,520,1024]{2,1,0:T(8,128)(2,1)S(1)}, bf16[1,520,1024]{2,1,0:T(8,128)(2,1)}, u32[]{:S(2)}) copy-start(bf16[1,520,1024]{2,1,0:T(8,128)(2,1)} %param.20) | copy-start | bytes 3194884
  15.1 44.1 %copy-start.100 = (s32[1,1040]{1,0:T(1,128)S(1)}, s32[1,1040]{1,0:T(1,128)}, u32[]{:S(2)}) copy-start(s32[1,1040]{1,0:T(1,128)} %param.21) | copy-start | bytes 12484
  15.1 478.8 %all-gather.19.cloned.1.call-start = ((), (), s32[]{:S(2)}) async-start(), calls=%async_computation.20 | async-start | bytes 9437184 | tf_op jit(solution)/shard_map/all_gather | solution.py:271
  15.8 706.5 %all-gather.21.cloned.1.call-start = ((), (), s32[]{:S(2)}) async-start(), calls=%async_computation.21 | async-start | bytes 18874368 | tf_op jit(solution)/shard_map/all_gather | solution.py:272
  16.4 1278.0 %reduce-scatter.11.cloned.1.call-start = ((), (), s32[]{:S(2)}) async-start(), calls=%async_computation.14 | async-start | bytes 9437184 | tf_op jit(solution)/shard_map/reduce_scatter | solution.py:292
  39.7 107.9 %copy-start.48 = (f32[1,1,1024]{2,0,1:T(1,128)}, f32[1,1,1024]{2,0,1:T(1,128)S(1)}, u32[]{:S(2)}) copy-start(f32[1,1,1024]{2,0,1:T(1,128)S(1)} %get-tuple-element.461) | copy-start | bytes 12292
  39.8 107.8 %copy-start.105 = (f32[1,1,1024]{2,0,1:T(1,128)}, f32[1,1,1024]{2,0,1:T(1,128)S(1)}, u32[]{:S(2)}) copy-start(f32[1,1,1024]{2,0,1:T(1,128)S(1)} %get-tuple-element.462) | copy-start | bytes 12292
  39.8 260.0 %copy-start.65 = (f32[1,1,1024]{2,0,1:T(1,128)}, f32[1,1,1024]{2,0,1:T(1,128)S(1)}, u32[]{:S(2)}) copy-start(f32[1,1,1024]{2,0,1:T(1,128)S(1)} %get-tuple-element.459) | copy-start | bytes 12292
  39.8 260.0 %copy-start.67 = (f32[1,1,1024]{2,0,1:T(1,128)}, f32[1,1,1024]{2,0,1:T(1,128)S(1)}, u32[]{:S(2)}) copy-start(f32[1,1,1024]{2,0,1:T(1,128)S(1)} %get-tuple-element.460) | copy-start | bytes 12292
  39.8 328.3 %copy-start.76 = (f32[1,1,1024]{2,0,1:T(1,128)}, f32[1,1,1024]{2,0,1:T(1,128)S(1)}, u32[]{:S(2)}) copy-start(f32[1,1,1024]{2,0,1:T(1,128)S(1)} %get-tuple-element.457) | copy-start | bytes 12292
  39.8 328.3 %copy-start.103 = (f32[1,1,1024]{2,0,1:T(1,128)}, f32[1,1,1024]{2,0,1:T(1,128)S(1)}, u32[]{:S(2)}) copy-start(f32[1,1,1024]{2,0,1:T(1,128)S(1)} %get-tuple-element.458) | copy-start | bytes 12292
  39.8 355.3 %copy-start.69 = (f32[1,1,1024]{2,0,1:T(1,128)}, f32[1,1,1024]{2,0,1:T(1,128)S(1)}, u32[]{:S(2)}) copy-start(f32[1,1,1024]{2,0,1:T(1,128)S(1)} %get-tuple-element.455) | copy-start | bytes 12292
  39.8 355.3 %copy-start.109 = (f32[1,1,1024]{2,0,1:T(1,128)}, f32[1,1,1024]{2,0,1:T(1,128)S(1)}, u32[]{:S(2)}) copy-start(f32[1,1,1024]{2,0,1:T(1,128)S(1)} %get-tuple-element.456) | copy-start | bytes 12292
  39.9 328.2 %copy-start.71 = (f32[1,4,1024]{2,0,1:T(1,128)}, f32[1,4,1024]{2,0,1:T(1,128)S(1)}, u32[]{:S(2)}) copy-start(f32[1,4,1024]{2,0,1:T(1,128)S(1)} %slice.263) | copy-start | bytes 49156
  58.7 88.9 %copy-start.41 = (f32[520]{0:T(1024)}, f32[520]{0:T(1024)S(1)}, u32[]{:S(2)}) copy-start(f32[520]{0:T(1024)S(1)} %broadcast_multiply_fusion.3) | copy-start | bytes 6244
  59.2 88.4 %copy-start.50 = (f32[520]{0:T(1024)}, f32[520]{0:T(1024)S(1)}, u32[]{:S(2)}) copy-start(f32[520]{0:T(1024)S(1)} %fusion.149) | copy-start | bytes 6244
  59.2 88.4 %copy-start.43 = (f32[520]{0:T(1024)}, f32[520]{0:T(1024)S(1)}, u32[]{:S(2)}) copy-start(f32[520]{0:T(1024)S(1)} %fusion.199) | copy-start | bytes 6244
  271.3 15.8 copy-start.15
  271.3 15.8 copy-start.39
  304.5 90.6 %copy-start.19 = (f32[1,520,1024]{2,1,0:T(8,128)}, f32[1,520,1024]{2,1,0:T(8,128)S(1)}, u32[]{:S(2)}) copy-start(f32[1,520,1024]{2,1,0:T(8,128)S(1)} %get-tuple-element.422) | copy-start | bytes 6389764
  304.5 90.6 %copy-start.56 = (f32[520]{0:T(1024)}, f32[520]{0:T(1024)S(1)}, u32[]{:S(2)}) copy-start(f32[520]{0:T(1024)S(1)} %broadcast_multiply_fusion.2) | copy-start | bytes 6244
  304.9 90.3 %copy-start.52 = (f32[520]{0:T(1024)}, f32[520]{0:T(1024)S(1)}, u32[]{:S(2)}) copy-start(f32[520]{0:T(1024)S(1)} %multiply_reduce_fusion.4) | copy-start | bytes 6244
  304.9 90.3 %copy-start.83 = (f32[520]{0:T(1024)}, f32[520]{0:T(1024)S(1)}, u32[]{:S(2)}) copy-start(f32[520]{0:T(1024)S(1)} %fusion.200) | copy-start | bytes 6244
  395.1 11.6 copy-start.118
  395.2 98.7 %copy-start.80 = (f32[1,1,1024]{2,0,1:T(1,128)S(1)}, f32[1,1,1024]{2,0,1:T(1,128)}, u32[]{:S(2)}) copy-start(f32[1,1,1024]{2,0,1:T(1,128)} %get-tuple-element.451) | copy-start | bytes 12292
  395.2 98.7 %copy-start.92 = (f32[3072]{0:T(1024)S(1)}, f32[3072]{0:T(1024)}, u32[]{:S(2)}) copy-start(f32[3072]{0:T(1024)} %get-tuple-element.471) | copy-start | bytes 36868
  395.2 98.7 %copy-start.107 = (f32[1,1,1024]{2,0,1:T(1,128)S(1)}, f32[1,1,1024]{2,0,1:T(1,128)}, u32[]{:S(2)}) copy-start(f32[1,1,1024]{2,0,1:T(1,128)} %get-tuple-element.452) | copy-start | bytes 12292
  406.7 241.0 %copy-start.5 = (f32[1,520,1024]{2,1,0:T(8,128)}, f32[1,520,1024]{2,1,0:T(8,128)S(1)}, u32[]{:S(2)}) copy-start(f32[1,520,1024]{2,1,0:T(8,128)S(1)} %get-tuple-element.418) | copy-start | bytes 6389764
  406.7 95.2 %copy-start.58 = (f32[520]{0:T(1024)}, f32[520]{0:T(1024)S(1)}, u32[]{:S(2)}) copy-start(f32[520]{0:T(1024)S(1)} %broadcast_multiply_fusion.1) | copy-start | bytes 6244
  407.1 94.9 %copy-start.54 = (f32[520]{0:T(1024)}, f32[520]{0:T(1024)S(1)}, u32[]{:S(2)}) copy-start(f32[520]{0:T(1024)S(1)} %multiply_reduce_fusion.3) | copy-start | bytes 6244
  407.1 94.8 %copy-start.85 = (f32[520]{0:T(1024)}, f32[520]{0:T(1024)S(1)}, u32[]{:S(2)}) copy-start(f32[520]{0:T(1024)S(1)} %fusion.201) | copy-start | bytes 6244
  621.7 13.0 copy-start.38
  621.7 13.0 copy-start.40
  647.7 74.6 %copy-start.73 = (f32[1,4,1024]{2,0,1:T(1,128)S(1)}, f32[1,4,1024]{2,0,1:T(1,128)}, u32[]{:S(2)}) copy-start(f32[1,4,1024]{2,0,1:T(1,128)} %slice.281) | copy-start | bytes 49156
  647.7 74.6 %copy-start.74 = (f32[1,1,1024]{2,0,1:T(1,128)S(1)}, f32[1,1,1024]{2,0,1:T(1,128)}, u32[]{:S(2)}) copy-start(f32[1,1,1024]{2,0,1:T(1,128)} %get-tuple-element.447) | copy-start | bytes 12292
  647.7 74.5 %copy-start.101 = (f32[1,1,1024]{2,0,1:T(1,128)S(1)}, f32[1,1,1024]{2,0,1:T(1,128)}, u32[]{:S(2)}) copy-start(f32[1,1,1024]{2,0,1:T(1,128)} %get-tuple-element.448) | copy-start | bytes 12292
  652.5 122.1 %copy-start.61 = (f32[520]{0:T(1024)}, f32[520]{0:T(1024)S(1)}, u32[]{:S(2)}) copy-start(f32[520]{0:T(1024)S(1)} %broadcast_multiply_fusion) | copy-start | bytes 6244
  654.3 120.2 %copy-start.88 = (f32[520]{0:T(1024)}, f32[520]{0:T(1024)S(1)}, u32[]{:S(2)}) copy-start(f32[520]{0:T(1024)S(1)} %fusion.202) | copy-start | bytes 6244
  722.3 28.1 %copy-start.34 = (bf16[1,520,1024]{2,1,0:T(8,128)(2,1)S(1)}, bf16[1,520,1024]{2,1,0:T(8,128)(2,1)}, u32[]{:S(2)}) copy-start(bf16[1,520,1024]{2,1,0:T(8,128)(2,1)} %param.25) | copy-start | bytes 3194884
  722.3 28.1 %copy-start.78 = (f32[1,1,1024]{2,0,1:T(1,128)S(1)}, f32[1,1,1024]{2,0,1:T(1,128)}, u32[]{:S(2)}) copy-start(f32[1,1,1024]{2,0,1:T(1,128)} %get-tuple-element.445) | copy-start | bytes 12292
  750.4 14.6 copy-start.9
  937.0 14.4 copy-start.70
  952.4 14.3 copy-start.37
  952.4 14.3 copy-start.20
  952.4 14.3 copy-start.57
  952.4 14.3 copy-start.77
  952.4 14.3 copy-start.84
  966.7 10.0 copy-start.120
  1147.2 299.7 %reduce-scatter.13.cloned.1.call-start = ((), (), s32[]{:S(2)}) async-start(), calls=%async_computation.15 | async-start | bytes 9437184 | tf_op jit(solution)/shard_map/reduce_scatter | solution.py:292
  1167.7 564.7 %reduce-scatter.15.cloned.1.call-start = ((), (), s32[]{:S(2)}) async-start(), calls=%async_computation.16 | async-start | bytes 18874368 | tf_op jit(solution)/shard_map/reduce_scatter | solution.py:295
  1193.2 825.2 %reduce-scatter.17.cloned.1.call-start = ((), (), s32[]{:S(2)}) async-start(), calls=%async_computation.17 | async-start | bytes 18874368 | tf_op jit(solution)/shard_map/reduce_scatter | solution.py:295
  1219.4 863.3 %reduce-scatter.19.cloned.1.call-start = ((), (), s32[]{:S(2)}) async-start(), calls=%async_computation.24 | async-start | bytes 294912
  1233.9 912.9 %reduce-scatter.21.cloned.1.call-start = ((), (), s32[]{:S(2)}) async-start(), calls=%async_computation.25 | async-start | bytes 294912
  1237.5 781.0 %copy-start.13 = (f32[520,1024]{1,0:T(8,128)S(1)}, f32[520,1024]{1,0:T(8,128)}, u32[]{:S(2)}) copy-start(f32[520,1024]{1,0:T(8,128)} %copy-done.12) | copy-start | bytes 6389764
  1237.5 781.0 %copy-start.18 = (bf16[1,520,1024]{2,1,0:T(8,128)(2,1)S(1)}, bf16[1,520,1024]{2,1,0:T(8,128)(2,1)}, u32[]{:S(2)}) copy-start(bf16[1,520,1024]{2,1,0:T(8,128)(2,1)} %param.20) | copy-start | bytes 3194884
  1237.5 944.4 %all-gather.23.cloned.1.call-start = ((), (), s32[]{:S(2)}) async-start(), calls=%async_computation.22 | async-start | bytes 5242880 | tf_op jit(solution)/shard_map/all_gather | solution.py:304
  1294.4 923.4 %all-gather.25.cloned.1.call-start = ((), (), s32[]{:S(2)}) async-start(), calls=%async_computation.23 | async-start | bytes 5242880 | tf_op jit(solution)/shard_map/all_gather | solution.py:304
  1446.9 859.1 %all-reduce.4.cloned.1.call-start = ((), (), s32[]{:S(2)}) async-start(), calls=%async_computation.26 | async-start | bytes 8388608 | tf_op jit(solution)/shard_map/psum | solution.py:308
  2018.5 134.9 %copy-start.46 = (bf16[2,14,128]{2,0,1:T(2,128)(2,1)S(1)}, bf16[2,14,128]{2,0,1:T(2,128)(2,1)}, u32[]{:S(2)}) copy-start(bf16[2,14,128]{2,0,1:T(2,128)(2,1)} %param.24) | copy-start | bytes 21508
  2018.5 134.9 %copy-start.90 = (f32[2,14,128]{2,0,1:T(2,128)S(1)}, f32[2,14,128]{2,0,1:T(2,128)}, u32[]{:S(2)}) copy-start(f32[2,14,128]{2,0,1:T(2,128)} %param.30) | copy-start | bytes 43012
  2018.5 134.9 %copy-start.91 = (f32[2,14,128]{2,0,1:T(2,128)S(1)}, f32[2,14,128]{2,0,1:T(2,128)}, u32[]{:S(2)}) copy-start(f32[2,14,128]{2,0,1:T(2,128)} %param.31) | copy-start | bytes 43012
  2185.0 37.1 %copy-start.27 = (bf16[2,128,4096]{2,1,0:T(8,128)(2,1)S(1)}, bf16[2,128,4096]{2,1,0:T(8,128)(2,1)}, u32[]{:S(2)}) copy-start(bf16[2,128,4096]{2,1,0:T(8,128)(2,1)} %param.22) | copy-start | bytes 6291460
  (84 other events, 373.0 us)
Sparse Core Ops, SparseCore 0:
  10.7 128.7 all-gather.14
  142.2 225.7 all-gather.16
  370.8 123.1 all-gather.18
  496.5 225.7 all-gather.20
  1147.3 147.0 reduce-scatter.10
  1298.9 147.9 reduce-scatter.12
  1450.7 281.6 reduce-scatter.14
  1736.6 281.7 reduce-scatter.16
  2022.3 60.3 reduce-scatter.18
  2086.5 60.2 reduce-scatter.20
  2148.4 33.4 all-gather.22
  2183.3 34.4 all-gather.24
  2220.3 85.6 all-reduce.3
